TPU v7x, 32 devices: a whole 2x2x4 slice. The times are simulated.
32 devices in a mesh: dp: 8 (over z, y), mp: 4 (over x, core).
Axes of the slice: x: 2, y: 2, z: 4, core: 2. Of those that a mesh axis runs over, the one named last changes fastest.
Arguments:
- tokens: bfloat16 [14592, 768], P(('dp', 'mp')), may hold values from -6 to 6
- caption_mask: int32 [64, 128], P('dp'), may hold values from 0 to 1, as said below
- region_counts: int32 [16], replicated, may hold values from 36 to 100, as said below
- group_ids: int32 [64], P('dp'), may hold values from 0 to 15, as said below
- query_weight: bfloat16 [768, 768], P(None, 'mp'), may hold values from -0.21875 to 0.21875
- query_bias: float32 [768], P('mp'), may hold values from -3 to 3
- key_weight: bfloat16 [768, 768], P(None, 'mp'), may hold values from -0.21875 to 0.21875
- value_weight: bfloat16 [768, 768], P(None, 'mp'), may hold values from -0.21875 to 0.21875
- value_bias: float32 [768], P('mp'), may hold values from -3 to 3
- out_weight: bfloat16 [768, 768], P('mp'), may hold values from -1.25 to 1.25
- out_bias: float32 [768], replicated, may hold values from -3 to 3
- attn_gain: float32 [768], replicated, may hold values from 0.5 to 1.5
- attn_shift: float32 [768], replicated, may hold values from -3 to 3
- up_weight: bfloat16 [768, 3072], P(None, 'mp'), may hold values from -0.21875 to 0.21875
- up_bias: float32 [3072], P('mp'), may hold values from -3 to 3
- down_weight: bfloat16 [3072, 768], P('mp'), may hold values from -0.109375 to 0.109375
- down_bias: float32 [768], replicated, may hold values from -3 to 3
- final_gain: float32 [768], replicated, may hold values from 0.5 to 1.5
- final_shift: float32 [768], replicated, may hold values from -3 to 3
- cotangent: bfloat16 [14592, 768], P(('dp', 'mp')), may hold values from -6 to 6
Outputs:
- layer_out: bfloat16 [14592, 768], P(('dp', 'mp'))
- grad_tokens: float32 [14592, 768], P(('dp', 'mp'))
- grad_query_weight: float32 [768, 768], P(None, 'mp')
- grad_query_bias: float32 [768], P('mp')
- grad_key_weight: float32 [768, 768], P(None, 'mp')
- grad_value_weight: float32 [768, 768], P(None, 'mp')
- grad_value_bias: float32 [768], P('mp')
- grad_out_weight: float32 [768, 768], P('mp')
- grad_out_bias: float32 [768], replicated
- grad_attn_gain: float32 [768], replicated
- grad_attn_shift: float32 [768], replicated
- grad_up_weight: float32 [768, 3072], P(None, 'mp')
- grad_up_bias: float32 [3072], P('mp')
- grad_down_weight: float32 [3072, 768], P('mp')
- grad_down_bias: float32 [768], replicated
- grad_final_gain: float32 [768], replicated
- grad_final_shift: float32 [768], replicated
Inputs may be any that keep to these rules, and one draw needn't show every extreme that they name: `caption_mask`: each row is ones followed by zeros, with at least one one; some row is all ones. `region_counts`: some image has exactly 100 regions. `group_ids`: each image is named by exactly 4 sequences.
All inputs are finite; a program needn't handle non-finite values.
Results may differ from a plain program's by a relative error of at most 0.015.
Values may be sent and summed in bfloat16 or wider, within the bound.
A program may use at most 128 MiB of HBM per device.

v0:
```python
import jax
import jax.numpy as jnp
from jax import lax
from jax.sharding import PartitionSpec as P

HEAD = 64
MAXREG = 100
EPS = 1e-12
ROOT_HALF = 0.7071067811865476
DENSITY = 0.3989422804014327
MASKED = -1e30


def key_valid(caption_mask, region_counts, group_ids):
    images = region_counts.shape[0]
    match = group_ids[:, None] == jnp.arange(images, dtype=jnp.int32)[None, :]
    regions = jnp.sum(jnp.where(match, region_counts[None, :], 0), axis=1)
    slots = jnp.arange(MAXREG, dtype=jnp.int32)
    return jnp.concatenate([caption_mask > 0, slots[None, :] < regions[:, None]], axis=1)


def norm_forward(total, gain, shift):
    mean = jnp.mean(total, axis=-1, keepdims=True)
    centered = total - mean
    inverse = lax.rsqrt(jnp.mean(centered * centered, axis=-1, keepdims=True) + EPS)
    scaled = centered * inverse
    return (scaled * gain + shift, scaled, inverse)


def norm_backward(grad, scaled, inverse, gain):
    weighted = grad * gain
    centered = weighted - jnp.mean(weighted, axis=-1, keepdims=True)
    return inverse * (centered - scaled * jnp.mean(weighted * scaled, axis=-1, keepdims=True))


def split_heads(block, seqs):
    return block.reshape(seqs, -1, block.shape[1] // HEAD, HEAD)


def masked_scores(query_heads, key_heads, valid):
    scores = jnp.einsum(
        "sqhd,skhd->shqk", query_heads, key_heads, preferred_element_type=jnp.float32
    ) * HEAD ** (-0.5)
    return jnp.where(valid[:, None, None, :], scores, MASKED)


def attend(query, keys, values, valid):
    seqs = valid.shape[0]
    value_heads = split_heads(values, seqs)
    scores = masked_scores(split_heads(query, seqs), split_heads(keys, seqs), valid)
    top = jnp.max(scores, axis=-1, keepdims=True)
    weights = jnp.exp(scores - top)
    total = jnp.sum(weights, axis=-1, keepdims=True)
    probs = (weights / total).astype(jnp.bfloat16)
    context = jnp.einsum("shqk,skhd->sqhd", probs, value_heads, preferred_element_type=jnp.float32)
    return (context.reshape(query.shape).astype(jnp.bfloat16), top + jnp.log(total))


def attend_backward(query, keys, values, valid, log_total, grad_context):
    seqs = valid.shape[0]
    query_heads = split_heads(query, seqs)
    key_heads = split_heads(keys, seqs)
    value_heads = split_heads(values, seqs)
    grad_heads = split_heads(grad_context, seqs)
    probs = jnp.exp(masked_scores(query_heads, key_heads, valid) - log_total)
    grad_values = jnp.einsum(
        "shqk,sqhd->skhd",
        probs.astype(jnp.bfloat16),
        grad_heads,
        preferred_element_type=jnp.float32,
    )
    grad_probs = jnp.einsum(
        "sqhd,skhd->shqk", grad_heads, value_heads, preferred_element_type=jnp.float32
    )
    row_total = jnp.sum(probs * grad_probs, axis=-1, keepdims=True)
    grad_scores = (probs * (grad_probs - row_total)).astype(jnp.bfloat16)
    scale = HEAD ** (-0.5)
    grad_query = (
        jnp.einsum("shqk,skhd->sqhd", grad_scores, key_heads, preferred_element_type=jnp.float32)
        * scale
    )
    grad_keys = (
        jnp.einsum("shqk,sqhd->skhd", grad_scores, query_heads, preferred_element_type=jnp.float32)
        * scale
    )
    shape = query.shape
    return (
        grad_query.reshape(shape).astype(jnp.bfloat16),
        grad_keys.reshape(shape).astype(jnp.bfloat16),
        grad_values.reshape(shape).astype(jnp.bfloat16),
    )


def attention_forward(
    tokens,
    valid,
    query_weight,
    query_bias,
    key_weight,
    value_weight,
    value_bias,
    out_weight,
    out_bias,
    attn_gain,
    attn_shift,
):
    whole = lax.all_gather(tokens, "mp", axis=0, tiled=True)
    query = (jnp.dot(whole, query_weight, preferred_element_type=jnp.float32) + query_bias).astype(
        jnp.bfloat16
    )
    keys = jnp.dot(whole, key_weight, preferred_element_type=jnp.float32).astype(jnp.bfloat16)
    values = (jnp.dot(whole, value_weight, preferred_element_type=jnp.float32) + value_bias).astype(
        jnp.bfloat16
    )
    context, log_total = attend(query, keys, values, valid)
    branch = lax.psum_scatter(
        jnp.dot(context, out_weight, preferred_element_type=jnp.float32),
        "mp",
        scatter_dimension=0,
        tiled=True,
    )
    normed, scaled, inverse = norm_forward(
        tokens.astype(jnp.float32) + branch + out_bias, attn_gain, attn_shift
    )
    return (whole, query, keys, values, context, log_total, normed, scaled, inverse)


def feedforward(normed, up_weight, up_bias, down_weight, down_bias, final_gain, final_shift):
    spread = lax.all_gather(normed.astype(jnp.bfloat16), "mp", axis=0, tiled=True)
    act_in = jnp.dot(spread, up_weight, preferred_element_type=jnp.float32) + up_bias
    cdf = 0.5 * (1.0 + jax.scipy.special.erf(act_in * ROOT_HALF))
    act = (act_in * cdf).astype(jnp.bfloat16)
    second = lax.psum_scatter(
        jnp.dot(act, down_weight, preferred_element_type=jnp.float32),
        "mp",
        scatter_dimension=0,
        tiled=True,
    )
    result, scaled, inverse = norm_forward(normed + second + down_bias, final_gain, final_shift)
    return (spread, act_in, act, result, scaled, inverse)


def body(
    tokens,
    caption_mask,
    region_counts,
    group_ids,
    query_weight,
    query_bias,
    key_weight,
    value_weight,
    value_bias,
    out_weight,
    out_bias,
    attn_gain,
    attn_shift,
    up_weight,
    up_bias,
    down_weight,
    down_bias,
    final_gain,
    final_shift,
    cotangent,
):
    valid = key_valid(caption_mask, region_counts, group_ids)
    first = attention_forward(
        tokens,
        valid,
        query_weight,
        query_bias,
        key_weight,
        value_weight,
        value_bias,
        out_weight,
        out_bias,
        attn_gain,
        attn_shift,
    )
    normed = first[6]
    second = feedforward(
        normed, up_weight, up_bias, down_weight, down_bias, final_gain, final_shift
    )
    layer_out = second[3].astype(jnp.bfloat16)
    second = feedforward(
        normed, up_weight, up_bias, down_weight, down_bias, final_gain, final_shift
    )
    spread, act_in, act, unused, scaled_out, inverse_out = second
    grad_out = cotangent.astype(jnp.float32)
    grad_final = norm_backward(grad_out, scaled_out, inverse_out, final_gain)
    final_gain_part = jnp.sum(grad_out * scaled_out, axis=0)
    final_shift_part = jnp.sum(grad_out, axis=0)
    grad_branch = lax.all_gather(grad_final.astype(jnp.bfloat16), "mp", axis=0, tiled=True)
    grad_down_weight = jnp.einsum("rf,rd->fd", act, grad_branch, preferred_element_type=jnp.float32)
    grad_down_bias = jnp.sum(grad_branch, axis=0, dtype=jnp.float32)
    grad_act = jnp.einsum("rd,fd->rf", grad_branch, down_weight, preferred_element_type=jnp.float32)
    cdf = 0.5 * (1.0 + jax.scipy.special.erf(act_in * ROOT_HALF))
    slope = cdf + act_in * jnp.exp(-0.5 * act_in * act_in) * DENSITY
    grad_in = (grad_act * slope).astype(jnp.bfloat16)
    grad_up_weight = jnp.einsum("rd,rf->df", spread, grad_in, preferred_element_type=jnp.float32)
    grad_up_bias = jnp.sum(grad_in, axis=0, dtype=jnp.float32)
    grad_mid = grad_final + lax.psum_scatter(
        jnp.einsum("rf,df->rd", grad_in, up_weight, preferred_element_type=jnp.float32),
        "mp",
        scatter_dimension=0,
        tiled=True,
    )
    upper_grads = (grad_up_weight, grad_up_bias, grad_down_weight, grad_down_bias)
    first = attention_forward(
        tokens,
        valid,
        query_weight,
        query_bias,
        key_weight,
        value_weight,
        value_bias,
        out_weight,
        out_bias,
        attn_gain,
        attn_shift,
    )
    whole, query, keys, values, context, log_total, unused_mid, scaled_mid, inverse_mid = first
    grad_first = norm_backward(grad_mid, scaled_mid, inverse_mid, attn_gain)
    attn_gain_part = jnp.sum(grad_mid * scaled_mid, axis=0)
    attn_shift_part = jnp.sum(grad_mid, axis=0)
    grad_attn = lax.all_gather(grad_first.astype(jnp.bfloat16), "mp", axis=0, tiled=True)
    grad_out_weight = jnp.einsum(
        "rc,rd->cd", context, grad_attn, preferred_element_type=jnp.float32
    )
    grad_out_bias = jnp.sum(grad_attn, axis=0, dtype=jnp.float32)
    grad_context = jnp.einsum(
        "rd,cd->rc", grad_attn, out_weight, preferred_element_type=jnp.float32
    ).astype(jnp.bfloat16)
    grad_query, grad_keys, grad_values = attend_backward(
        query, keys, values, valid, log_total, grad_context
    )
    grad_query_weight = jnp.einsum(
        "rd,rc->dc", whole, grad_query, preferred_element_type=jnp.float32
    )
    grad_query_bias = jnp.sum(grad_query, axis=0, dtype=jnp.float32)
    grad_key_weight = jnp.einsum("rd,rc->dc", whole, grad_keys, preferred_element_type=jnp.float32)
    grad_value_weight = jnp.einsum(
        "rd,rc->dc", whole, grad_values, preferred_element_type=jnp.float32
    )
    grad_value_bias = jnp.sum(grad_values, axis=0, dtype=jnp.float32)
    total = jnp.einsum("rc,dc->rd", grad_query, query_weight, preferred_element_type=jnp.float32)
    total = total + jnp.einsum(
        "rc,dc->rd", grad_keys, key_weight, preferred_element_type=jnp.float32
    )
    grad_tokens = grad_first + lax.psum_scatter(
        (
            total
            + jnp.einsum("rc,dc->rd", grad_values, value_weight, preferred_element_type=jnp.float32)
        ).astype(jnp.bfloat16),
        "mp",
        scatter_dimension=0,
        tiled=True,
    ).astype(jnp.float32)
    norm_sums = lax.psum(
        (attn_gain_part, attn_shift_part, final_gain_part, final_shift_part), ("dp", "mp")
    )
    summed = lax.psum(
        (
            grad_query_weight,
            grad_query_bias,
            grad_key_weight,
            grad_value_weight,
            grad_value_bias,
            grad_out_weight,
            grad_out_bias,
            grad_up_weight,
            grad_up_bias,
            grad_down_weight,
            grad_down_bias,
        ),
        "dp",
    )
    lower_grads = summed[:7]
    upper_grads = summed[7:]
    return (
        layer_out,
        grad_tokens,
        lower_grads[0],
        lower_grads[1],
        lower_grads[2],
        lower_grads[3],
        lower_grads[4],
        lower_grads[5],
        lower_grads[6],
        norm_sums[0],
        norm_sums[1],
        upper_grads[0],
        upper_grads[1],
        upper_grads[2],
        upper_grads[3],
        norm_sums[2],
        norm_sums[3],
    )


def solution(mesh):
    return jax.shard_map(
        body,
        mesh=mesh,
        in_specs=(
            P(("dp", "mp"), None),
            P("dp", None),
            P(),
            P("dp"),
            P(None, "mp"),
            P("mp"),
            P(None, "mp"),
            P(None, "mp"),
            P("mp"),
            P("mp", None),
            P(),
            P(),
            P(),
            P(None, "mp"),
            P("mp"),
            P("mp", None),
            P(),
            P(),
            P(),
            P(("dp", "mp"), None),
        ),
        out_specs=(
            P(("dp", "mp"), None),
            P(("dp", "mp"), None),
            P(None, "mp"),
            P("mp"),
            P(None, "mp"),
            P(None, "mp"),
            P("mp"),
            P("mp", None),
            P(),
            P(),
            P(),
            P(None, "mp"),
            P("mp"),
            P("mp", None),
            P(),
            P(),
            P(),
        ),
        check_vma=False,
    )
```

profile of v0, /device:TPU:0, one launch (start us, length us, event | category | flops | bytes accessed | tf_op | source)
XLA Modules:
  0.0 669.5 jit_solution(431593237311319448)
XLA Ops:
  9.6 29.3 %all-gather.5.cloned.1.call-done = bf16[1824,768]{1,0:T(8,128)(2,1)} async-done(((bf16[456,768]{1,0:T(8,128)(2,1)}), bf16[1824,768]{1,0:T(8,128)(2,1)}) %all-gather.5.cloned.1.call-update) | async-done | bytes 2801680 | tf_op jit(solution)/shard_map/all_gather | solution.py:107
  38.9 2.9 convolution_convert_fusion.1
  43.2 3.2 fusion.13
  47.7 4.1 fusion.12
  51.8 2.5 reshape.127
  54.4 1.8 fusion.43
  61.3 4.4 fusion.44
  65.8 53.7 %reduce-scatter.5.cloned.1.call-done = f32[456,768]{1,0:T(8,128)} async-done(((f32[1824,768]{1,0:T(8,128)}), f32[456,768]{1,0:T(8,128)}) %reduce-scatter.5.cloned.1.call-update) | async-done | bytes 1400848 | tf_op jit(solution)/shard_map/reduce_scatter | solution.py:116
  119.5 1.8 fusion.42
  123.3 26.2 %all-gather.7.cloned.1.call-done = bf16[1824,768]{1,0:T(8,128)(2,1)} async-done(((bf16[456,768]{1,0:T(8,128)(2,1)}), bf16[1824,768]{1,0:T(8,128)(2,1)}) %all-gather.7.cloned.1.call-update) | async-done | bytes 2801680 | tf_op jit(solution)/shard_map/all_gather | solution.py:129
  149.5 6.4 multiply_convert_fusion.1
  155.9 1.6 copy-done.39
  157.5 4.8 fusion.45
  162.4 53.8 %reduce-scatter.7.cloned.1.call-done = f32[456,768]{1,0:T(8,128)} async-done(((f32[1824,768]{1,0:T(8,128)}), f32[456,768]{1,0:T(8,128)}) %reduce-scatter.7.cloned.1.call-update) | async-done | bytes 1400848 | tf_op jit(solution)/shard_map/reduce_scatter | solution.py:133
  216.1 1.9 fusion.41
  220.6 26.7 %all-gather.9.cloned.1.call-done = bf16[1824,768]{1,0:T(8,128)(2,1)} async-done(((bf16[456,768]{1,0:T(8,128)(2,1)}), bf16[1824,768]{1,0:T(8,128)(2,1)}) %all-gather.9.cloned.1.call-update) | async-done | bytes 2801680 | tf_op jit(solution)/shard_map/all_gather | solution.py:192
  247.2 6.3 convert_reduce_fusion.1
  253.5 1.6 copy-done.40
  255.2 4.9 fusion.46
  260.1 53.8 %reduce-scatter.9.cloned.1.call-done = f32[456,768]{1,0:T(8,128)} async-done(((f32[1824,768]{1,0:T(8,128)}), f32[456,768]{1,0:T(8,128)}) %reduce-scatter.9.cloned.1.call-update) | async-done | bytes 1400848 | tf_op jit(solution)/shard_map/reduce_scatter | solution.py:201
  313.9 3.8 multiply_reduce_fusion.1
  317.7 1.8 fusion.39
  319.7 26.4 %all-gather.11.cloned.1.call-done = bf16[1824,768]{1,0:T(8,128)(2,1)} async-done(((bf16[456,768]{1,0:T(8,128)(2,1)}), bf16[1824,768]{1,0:T(8,128)(2,1)}) %all-gather.11.cloned.1.call-update) | async-done | bytes 2801680 | tf_op jit(solution)/shard_map/all_gather | solution.py:225
  346.2 2.9 convolution_convert_fusion
  350.4 3.9 convert_reduce_fusion.4
  354.4 4.4 multiply_reduce_fusion
  360.3 1.9 fusion.26
  362.2 1.5 convert_reduce_fusion.5
  364.1 1.8 convert_element_type.144
  365.9 1.6 copy.74
  368.5 2.5 copy.77
  370.9 2.1 convert_element_type.140
  375.3 2.5 add_convert_fusion
  377.9 6.9 %fusion.51 = f32[768,768]{1,0:T(8,128)} fusion(bf16[1824,768]{1,0:T(8,128)(2,1)} %copy-done.39, bf16[1824,768]{1,0:T(8,128)(2,1)} %all-gather.9.cloned.1.call-done), kind=kOutput, calls=%fused_computation.101 | convolution fusion | flops 2151677952 | bytes 7962624 | tf_op jit(solution)/shard_map/rf,rd->fd/dot_general | solution.py:193
  384.8 4.1 fusion.50
  388.9 1.6 fusion.49
  391.0 1.6 convolution_bitcast_fusion
  392.7 1.6 convolution_bitcast_fusion.1
  394.3 1.6 convolution_bitcast_fusion.2
  395.9 2.4 convert_reduce_fusion
  398.3 41.6 %all-reduce = (f32[768]{0:T(1024)}, f32[768]{0:T(1024)}, f32[768]{0:T(1024)}, f32[768]{0:T(1024)}) all-reduce(f32[768]{0:T(1024)S(1)} %get-tuple-element.17, f32[768]{0:T(1024)S(1)} %get-tuple-element.22, f32[768]{0:T(1024)S(1)} %get-tuple-element.19, f32[768]{0:T(1024)S(1)} %get-tuple-element.24), channel_id=1, replica_groups=mesh['dp'=8,'mp'=4] {'dp','mp'}, use_global_device_ids=true, to_apply=%region_27.28 | all-reduce | flops 3072 | bytes 24576 | tf_op jit(solution)/shard_map/psum | solution.py:258
  440.0 2.3 convert_reduce_fusion.2
  442.3 39.6 %all-reduce.1 = (f32[192]{0:T(256)}, f32[192]{0:T(256)}, f32[768]{0:T(1024)}, f32[768]{0:T(1024)}, f32[768]{0:T(1024)}) all-reduce(f32[192]{0:T(256)S(1)} %reduce_sum.216, f32[192]{0:T(256)S(1)} %reduce_sum.218, f32[768]{0:T(1024)S(1)} %convert_reduce_fusion.2, ...), channel_id=1, replica_groups=mesh['dp'=8,'mp'=4] {'dp'}, use_global_device_ids=true, to_apply=%region_18.19 | all-reduce | flops 2688 | bytes 21504 | tf_op jit(solution)/shard_map/psum | solution.py:261
  482.0 2.3 convert_add_fusion
  484.3 168.9 %all-reduce.5.cloned.1.call-done = (f32[768,192]{0,1:T(8,128)}, f32[768,192]{0,1:T(8,128)}, f32[768,192]{0,1:T(8,128)}, f32[192,768]{1,0:T(8,128)}, f32[768,768]{1,0:T(8,128)}, /*index=5*/f32[768,768]{1,0:T(8,128)}) async-done(((f32[768,192]{0,1:T(8,128)}, f32[768,192]{0,1:T(8,128)}, f32[768,192]{0,1:T(8,128)}, f32[192,768]{1,0:T(8,128)}, f32[768,768]{1,0:T(8,128)}, /*index=5*/f32[768,768]{1,0:T(8,128)}), ...) | async-done | bytes 7077904 | tf_op jit(solution)/shard_map/psum | solution.py:261
  653.2 2.1 copy.119
  655.2 1.9 copy.120
  657.2 1.9 copy.121
  (140 shorter events, 25.6 us)
Async XLA Ops:
  7.2 142.3 %copy-start = (bf16[768,768]{1,0:T(8,128)(2,1)S(1)}, bf16[768,768]{1,0:T(8,128)(2,1)}, u32[]{:S(2)}) copy-start(bf16[768,768]{1,0:T(8,128)(2,1)} %param.33) | copy-start | bytes 3538948
  7.2 31.7 %all-gather.5.cloned.1.call-start = ((), (), s32[]{:S(2)}) async-start(), calls=%async_computation.4 | async-start | bytes 3502080 | tf_op jit(solution)/shard_map/all_gather | solution.py:107
  7.9 111.6 %reduce-scatter.5.cloned.1.call-start = ((), (), s32[]{:S(2)}) async-start(), calls=%async_computation.5 | async-start | bytes 7004160 | tf_op jit(solution)/shard_map/reduce_scatter | solution.py:116
  9.6 33.5 %copy-start.37 = (f32[192]{0:T(256)S(1)}, f32[192]{0:T(256)}, u32[]{:S(2)}) copy-start(f32[192]{0:T(256)} %param.25) | copy-start | bytes 2308
  43.1 11.2 %copy-start.6 = (bf16[8,228,3,64]{1,0,3,2:T(8,128)(2,1)}, bf16[8,228,3,64]{1,0,3,2:T(8,128)(2,1)S(1)}, u32[]{:S(2)}) copy-start(bf16[8,228,3,64]{1,0,3,2:T(8,128)(2,1)S(1)} %reshape.129) | copy-start | bytes 2101252
  43.1 4.6 copy-start.38
  47.7 6.6 copy-start.8
  54.3 2.8 copy-start.15
  56.2 2.5 copy-start.2
  56.2 2.5 copy-start.20
  65.7 53.8 %copy-start.31 = (f32[768]{0:T(1024)S(1)}, f32[768]{0:T(1024)}, u32[]{:S(2)}) copy-start(f32[768]{0:T(1024)} %param.30) | copy-start | bytes 9220
  65.7 55.9 %copy-start.28 = (f32[768]{0:T(1024)S(1)}, f32[768]{0:T(1024)}, u32[]{:S(2)}) copy-start(f32[768]{0:T(1024)} %param.31) | copy-start | bytes 9220
  65.7 55.9 %copy-start.30 = (f32[768]{0:T(1024)S(1)}, f32[768]{0:T(1024)}, u32[]{:S(2)}) copy-start(f32[768]{0:T(1024)} %param.32) | copy-start | bytes 9220
  65.7 83.8 %all-gather.7.cloned.1.call-start = ((), (), s32[]{:S(2)}) async-start(), calls=%async_computation.6 | async-start | bytes 3502080 | tf_op jit(solution)/shard_map/all_gather | solution.py:129
  121.3 28.2 %copy-start.36 = (f32[768]{0:T(1024)S(1)}, f32[768]{0:T(1024)}, u32[]{:S(2)}) copy-start(f32[768]{0:T(1024)} %param.34) | copy-start | bytes 9220
  122.8 93.3 %reduce-scatter.7.cloned.1.call-start = ((), (), s32[]{:S(2)}) async-start(), calls=%async_computation.7 | async-start | bytes 7004160 | tf_op jit(solution)/shard_map/reduce_scatter | solution.py:133
  149.5 7.9 %copy-start.35 = (bf16[768,768]{1,0:T(8,128)(2,1)S(1)}, bf16[768,768]{1,0:T(8,128)(2,1)}, u32[]{:S(2)}) copy-start(bf16[768,768]{1,0:T(8,128)(2,1)} %param.35) | copy-start | bytes 3538948
  155.9 1.6 copy-start.39
  162.3 53.8 %copy-start.33 = (f32[768]{0:T(1024)S(1)}, f32[768]{0:T(1024)}, u32[]{:S(2)}) copy-start(f32[768]{0:T(1024)} %param.36) | copy-start | bytes 9220
  162.3 56.1 %copy-start.29 = (f32[768]{0:T(1024)S(1)}, f32[768]{0:T(1024)}, u32[]{:S(2)}) copy-start(f32[768]{0:T(1024)} %param.37) | copy-start | bytes 9220
  162.3 84.9 %all-gather.9.cloned.1.call-start = ((), (), s32[]{:S(2)}) async-start(), calls=%async_computation.8 | async-start | bytes 3502080 | tf_op jit(solution)/shard_map/all_gather | solution.py:192
  216.1 2.3 copy-start.12
  220.5 93.4 %reduce-scatter.9.cloned.1.call-start = ((), (), s32[]{:S(2)}) async-start(), calls=%async_computation.9 | async-start | bytes 7004160 | tf_op jit(solution)/shard_map/reduce_scatter | solution.py:201
  253.5 1.6 copy-start.40
  260.0 53.8 %copy-start.13 = (bf16[456,768]{1,0:T(8,128)(2,1)S(1)}, bf16[456,768]{1,0:T(8,128)(2,1)}, u32[]{:S(2)}) copy-start(bf16[456,768]{1,0:T(8,128)(2,1)} %param.39) | copy-start | bytes 2101252
  260.0 53.8 %copy-start.32 = (f32[768]{0:T(1024)S(1)}, f32[768]{0:T(1024)}, u32[]{:S(2)}) copy-start(f32[768]{0:T(1024)} %param.38) | copy-start | bytes 9220
  260.1 86.1 %all-gather.11.cloned.1.call-start = ((), (), s32[]{:S(2)}) async-start(), calls=%async_computation.10 | async-start | bytes 3502080 | tf_op jit(solution)/shard_map/all_gather | solution.py:225
  317.7 2.0 copy-start.21
  317.7 2.0 copy-start.27
  317.7 28.5 %copy-start.22 = (bf16[192,768]{1,0:T(8,128)(2,1)S(1)}, bf16[192,768]{1,0:T(8,128)(2,1)}, u32[]{:S(2)}) copy-start(bf16[192,768]{1,0:T(8,128)(2,1)} %param.29) | copy-start | bytes 884740
  319.5 162.5 %reduce-scatter.11.cloned.1.call-start = ((), (), s32[]{:S(2)}) async-start(), calls=%async_computation.11 | async-start | bytes 3502080 | tf_op jit(solution)/shard_map/reduce_scatter | solution.py:249
  350.4 4.0 copy-start.16
  350.4 8.4 %slice-start = ((s8[5701632]{0:T(1024)(128)(4,1)}), s8[4194304]{0:T(1024)(128)(4,1)S(1)}, s32[]{:S(2)}) async-start(s8[5701632]{0:T(1024)(128)(4,1)} %bitcast.74), calls=%async_computation.13 | async-start | bytes 8388608
  354.4 4.5 slice-start.1
  358.9 1.4 copy-start.9
  360.3 1.9 copy-start.7
  365.9 7.1 %copy-start.23 = (bf16[768,192]{0,1:T(8,128)(2,1)S(1)}, bf16[768,192]{0,1:T(8,128)(2,1)}, u32[]{:S(2)}) copy-start(bf16[768,192]{0,1:T(8,128)(2,1)} %param.24) | copy-start | bytes 884740
  377.8 275.3 %all-reduce.5.cloned.1.call-start = ((), (), s32[]{:S(2)}) async-start(), calls=%async_computation.12 | async-start | bytes 14155776 | tf_op jit(solution)/shard_map/psum | solution.py:261
  377.9 6.9 %copy-start.34 = (bf16[1824,768]{1,0:T(8,128)(2,1)S(1)}, bf16[1824,768]{1,0:T(8,128)(2,1)}, u32[]{:S(2)}) copy-start(bf16[1824,768]{1,0:T(8,128)(2,1)} %all-gather.7.cloned.1.call-done) | copy-start | bytes 8404996
  377.9 6.9 %copy-start.41 = (bf16[1824,768]{1,0:T(8,128)(2,1)S(1)}, bf16[1824,768]{1,0:T(8,128)(2,1)}, u32[]{:S(2)}) copy-start(bf16[1824,768]{1,0:T(8,128)(2,1)} %copy-done.40) | copy-start | bytes 8404996
  384.8 4.1 copy-start.5
  388.9 1.8 copy-start.4
  388.9 2.2 copy-start.11
  395.9 86.1 %copy-start.14 = (f32[456,768]{1,0:T(8,128)S(1)}, f32[456,768]{1,0:T(8,128)}, u32[]{:S(2)}) copy-start(f32[456,768]{1,0:T(8,128)} %get-tuple-element.41) | copy-start | bytes 4202500
  653.2 5.9 copy-start.19
  653.2 6.7 %copy-start.18 = (f32[768,768]{1,0:T(8,128)S(1)}, f32[768,768]{1,0:T(8,128)}, u32[]{:S(2)}) copy-start(f32[768,768]{1,0:T(8,128)} %get-tuple-element.73) | copy-start | bytes 7077892
  659.1 2.2 copy-start.17
  659.9 2.8 copy-start.1
  (5 other events, 5.6 us)
Sparse Core Ops, SparseCore 0:
  9.6 29.2 all-gather.4
  65.8 53.6 reduce-scatter.4
  122.9 26.5 all-gather.6
  162.4 53.6 reduce-scatter.6
  220.6 26.5 all-gather.8
  260.2 53.6 reduce-scatter.8
  319.6 26.5 all-gather.10
  377.9 36.2 reduce-scatter.10
  420.5 232.6 all-reduce.4
where the time goes:
time: 678 us; the launch traced here: 669 us
  waiting for transfers between devices  440 us (65%)
  blocking collectives  81.2 us (12%)
  matrix products  76.6 us (11%)
  local copies, waits for them, and re-layouts  32.5 us (5%)
  other arithmetic  24 us (4%)
  between operations  14.7 us (2%)
    psum x1, waiting for transfers between devices, body(): lax.psum((grad_query_weight, grad_query_bias, grad_key_weight, grad_value...  169 us
    reduce_scatter x1, waiting for transfers between devices, body(): lax.psum_scatter(jnp.einsum('rf,df->rd', grad_in, up_weight, preferred_el...  53.8 us
    reduce_scatter x1, waiting for transfers between devices, feedforward(): lax.psum_scatter(jnp.dot(act, down_weight, preferred_element_type=jnp.flo...  53.8 us
    reduce_scatter x1, waiting for transfers between devices, attention_forward(): lax.psum_scatter(jnp.dot(context, out_weight, preferred_element_type=jnp....  53.7 us
    psum x1, blocking collectives, body(): lax.psum((attn_gain_part, attn_shift_part, final_gain_part, final_shift_p...  41.6 us
    psum x1, blocking collectives, body(): lax.psum((grad_query_weight, grad_query_bias, grad_key_weight, grad_value...  39.6 us
    all_gather x1, waiting for transfers between devices, attention_forward(): whole = lax.all_gather(tokens, 'mp', axis=0, tiled=True)  29.3 us
    all_gather x1, waiting for transfers between devices, body(): lax.all_gather(grad_final.astype(jnp.bfloat16), 'mp', axis=0, tiled=True)  26.7 us
  transfers between devices with their start and end apart: 9, of which 8 were waited for; matrix products, arithmetic and copies ran while one was open for 4% of the time, Pallas kernels for 0%

commit v1 on v0

--- a/solution.py
+++ b/solution.py
@@ -9,6 +9,27 @@
 ROOT_HALF = 0.7071067811865476
 DENSITY = 0.3989422804014327
 MASKED = -1e30
+
+
+def collect(x, axis, dim):
+    count, place, width = (lax.axis_size(axis), lax.axis_index(axis), x.shape[dim])
+    upward = [(i, (i + 1) % count) for i in range(count)]
+    left = [(i, (i - 1) % count) for i in range(count)]
+    out = jnp.zeros((*x.shape[:dim], count * width, *x.shape[dim + 1 :]), x.dtype)
+    out = lax.dynamic_update_slice_in_dim(out, x, place * width, axis=dim)
+    from_left = from_right = x
+    half = count // 2
+    for lap in range(1, half + 1):
+        from_left = lax.ppermute(from_left, axis, upward)
+        out = lax.dynamic_update_slice_in_dim(
+            out, from_left, (place - lap) % count * width, axis=dim
+        )
+        if lap < count - half:
+            from_right = lax.ppermute(from_right, axis, left)
+            out = lax.dynamic_update_slice_in_dim(
+                out, from_right, (place + lap) % count * width, axis=dim
+            )
+    return out
 
 
 def key_valid(caption_mask, region_counts, group_ids):
@@ -104,7 +125,7 @@
     attn_gain,
     attn_shift,
 ):
-    whole = lax.all_gather(tokens, "mp", axis=0, tiled=True)
+    whole = collect(tokens, "mp", 0)
     query = (jnp.dot(whole, query_weight, preferred_element_type=jnp.float32) + query_bias).astype(
         jnp.bfloat16
     )

time: 678 us -> 678 us (level)
  waiting for transfers between devices: 440 us -> 433 us
    all_gather x1 -> x0, waiting for transfers between devices: 29.3 us -> none  [attention_forward(): whole = lax.all_gather(tokens, 'mp', axis=0, tiled=True)]
    ppermute x0 -> x3, waiting for transfers between devices: none -> 19.7 us  [the longest x2 19.7 us: collect(): from_left = lax.ppermute(from_left, axis, upward)]
    unnamed x94 -> x100, local copies, waits for them, and re-layouts: 15.2 us -> 16.4 us
  transfers between devices with their start and end apart: 9 -> 11, of which waited for: 8 -> 9; matrix products, arithmetic and copies ran while one was open for 4% -> 4% of each run, Pallas kernels for 0% -> 0%
where the time goes in v1:
time: 678 us; the launch traced here: 669 us
  waiting for transfers between devices  433 us (64%)
  blocking collectives  81.4 us (12%)
  matrix products  74.9 us (11%)
  local copies, waits for them, and re-layouts  34.1 us (5%)
  other arithmetic  24 us (4%)
  between operations  15 us (2%)
    psum x1, waiting for transfers between devices, body(): lax.psum((grad_query_weight, grad_query_bias, grad_key_weight, grad_value...  169 us
    reduce_scatter x1, waiting for transfers between devices, attention_forward(): lax.psum_scatter(jnp.dot(context, out_weight, preferred_element_type=jnp....  57.6 us
    reduce_scatter x1, waiting for transfers between devices, body(): lax.psum_scatter(jnp.einsum('rf,df->rd', grad_in, up_weight, preferred_el...  53.8 us
    reduce_scatter x1, waiting for transfers between devices, feedforward(): lax.psum_scatter(jnp.dot(act, down_weight, preferred_element_type=jnp.flo...  53.8 us
    psum x1, blocking collectives, body(): lax.psum((attn_gain_part, attn_shift_part, final_gain_part, final_shift_p...  41.8 us
    psum x1, blocking collectives, body(): lax.psum((grad_query_weight, grad_query_bias, grad_key_weight, grad_value...  39.5 us
    all_gather x1, waiting for transfers between devices, body(): lax.all_gather(grad_final.astype(jnp.bfloat16), 'mp', axis=0, tiled=True)  26.7 us
    all_gather x1, waiting for transfers between devices, body(): lax.all_gather(grad_first.astype(jnp.bfloat16), 'mp', axis=0, tiled=True)  26.4 us
  transfers between devices with their start and end apart: 11, of which 9 were waited for; matrix products, arithmetic and copies ran while one was open for 4% of the time, Pallas kernels for 0%

profile of v1, /device:TPU:0, one launch (start us, length us, event | category | flops | bytes accessed | tf_op | source)
XLA Modules:
  0.0 668.7 jit_solution(8141649928214548566)
XLA Ops:
  7.8 2.0 collective-permute-start.1
  11.3 12.3 %collective-permute-done = bf16[456,768]{1,0:T(8,128)(2,1)S(1)} collective-permute-done((bf16[456,768]{1,0:T(8,128)(2,1)}, bf16[456,768]{1,0:T(8,128)(2,1)S(1)}, u32[]{:S(2)}, u32[]{:S(2)}) %collective-permute-start) | collective-permute-done | bytes 700448 | tf_op jit(solution)/shard_map/ppermute | solution.py:23
  23.6 2.6 collective-permute-start.2
  26.6 7.4 %collective-permute-done.2 = bf16[456,768]{1,0:T(8,128)(2,1)S(1)} collective-permute-done((bf16[456,768]{1,0:T(8,128)(2,1)S(1)}, bf16[456,768]{1,0:T(8,128)(2,1)S(1)}, u32[]{:S(2)}, u32[]{:S(2)}) %collective-permute-start.2) | collective-permute-done | bytes 700448 | tf_op jit(solution)/shard_map/ppermute | solution.py:23
  38.2 3.2 fusion.13
  42.7 4.1 fusion.12
  46.8 2.5 reshape.127
  49.4 1.8 fusion.43
  56.3 4.4 fusion.44
  60.8 57.6 %reduce-scatter.5.cloned.1.call-done = f32[456,768]{1,0:T(8,128)} async-done(((f32[1824,768]{1,0:T(8,128)}), f32[456,768]{1,0:T(8,128)}) %reduce-scatter.5.cloned.1.call-update) | async-done | bytes 1400848 | tf_op jit(solution)/shard_map/reduce_scatter | solution.py:137
  118.4 1.8 fusion.42
  122.2 26.2 %all-gather.4.cloned.1.call-done = bf16[1824,768]{1,0:T(8,128)(2,1)} async-done(((bf16[456,768]{1,0:T(8,128)(2,1)}), bf16[1824,768]{1,0:T(8,128)(2,1)}) %all-gather.4.cloned.1.call-update) | async-done | bytes 2801680 | tf_op jit(solution)/shard_map/all_gather | solution.py:150
  148.4 6.4 multiply_convert_fusion.1
  156.3 4.8 fusion.45
  161.2 53.8 %reduce-scatter.7.cloned.1.call-done = f32[456,768]{1,0:T(8,128)} async-done(((f32[1824,768]{1,0:T(8,128)}), f32[456,768]{1,0:T(8,128)}) %reduce-scatter.7.cloned.1.call-update) | async-done | bytes 1400848 | tf_op jit(solution)/shard_map/reduce_scatter | solution.py:154
  215.0 1.9 fusion.41
  219.4 26.7 %all-gather.6.cloned.1.call-done = bf16[1824,768]{1,0:T(8,128)(2,1)} async-done(((bf16[456,768]{1,0:T(8,128)(2,1)}), bf16[1824,768]{1,0:T(8,128)(2,1)}) %all-gather.6.cloned.1.call-update) | async-done | bytes 2801680 | tf_op jit(solution)/shard_map/all_gather | solution.py:213
  246.1 6.3 convert_reduce_fusion.1
  252.4 1.6 copy-done.43
  254.0 4.9 fusion.46
  259.0 53.8 %reduce-scatter.9.cloned.1.call-done = f32[456,768]{1,0:T(8,128)} async-done(((f32[1824,768]{1,0:T(8,128)}), f32[456,768]{1,0:T(8,128)}) %reduce-scatter.9.cloned.1.call-update) | async-done | bytes 1400848 | tf_op jit(solution)/shard_map/reduce_scatter | solution.py:222
  312.8 3.8 multiply_reduce_fusion.1
  316.6 1.8 fusion.39
  318.6 26.4 %all-gather.8.cloned.1.call-done = bf16[1824,768]{1,0:T(8,128)(2,1)} async-done(((bf16[456,768]{1,0:T(8,128)(2,1)}), bf16[1824,768]{1,0:T(8,128)(2,1)}) %all-gather.8.cloned.1.call-update) | async-done | bytes 2801680 | tf_op jit(solution)/shard_map/all_gather | solution.py:246
  345.1 2.9 convolution_convert_fusion
  349.3 3.9 convert_reduce_fusion.4
  353.3 4.4 multiply_reduce_fusion
  359.2 1.9 fusion.26
  363.0 1.8 convert_element_type.144
  364.8 1.6 copy.74
  367.4 2.5 copy.77
  369.8 2.1 convert_element_type.140
  374.2 2.5 add_convert_fusion
  376.8 6.9 %fusion.51 = f32[768,768]{1,0:T(8,128)} fusion(bf16[1824,768]{1,0:T(8,128)(2,1)} %copy-done.42, bf16[1824,768]{1,0:T(8,128)(2,1)} %all-gather.6.cloned.1.call-done), kind=kOutput, calls=%fused_computation.102 | convolution fusion | flops 2151677952 | bytes 7962624 | tf_op jit(solution)/shard_map/rf,rd->fd/dot_general | solution.py:214
  383.7 4.1 fusion.50
  387.8 1.6 fusion.54
  389.4 1.6 fusion.53
  391.0 1.6 fusion.52
  392.8 1.6 fusion.49
  394.5 2.4 convert_reduce_fusion
  396.9 41.8 %all-reduce = (f32[768]{0:T(1024)}, f32[768]{0:T(1024)}, f32[768]{0:T(1024)}, f32[768]{0:T(1024)}) all-reduce(f32[768]{0:T(1024)S(1)} %get-tuple-element.17, f32[768]{0:T(1024)S(1)} %get-tuple-element.22, f32[768]{0:T(1024)S(1)} %get-tuple-element.19, f32[768]{0:T(1024)S(1)} %get-tuple-element.24), channel_id=1, replica_groups=mesh['dp'=8,'mp'=4] {'dp','mp'}, use_global_device_ids=true, to_apply=%region_27.28 | all-reduce | flops 3072 | bytes 24576 | tf_op jit(solution)/shard_map/psum | solution.py:279
  438.8 2.3 convert_reduce_fusion.2
  441.2 39.5 %all-reduce.1 = (f32[192]{0:T(256)}, f32[192]{0:T(256)}, f32[768]{0:T(1024)}, f32[768]{0:T(1024)}, f32[768]{0:T(1024)}) all-reduce(f32[192]{0:T(256)S(1)} %reduce_sum.216, f32[192]{0:T(256)S(1)} %reduce_sum.218, f32[768]{0:T(1024)S(1)} %convert_reduce_fusion.2, ...), channel_id=1, replica_groups=mesh['dp'=8,'mp'=4] {'dp'}, use_global_device_ids=true, to_apply=%region_18.19 | all-reduce | flops 2688 | bytes 21504 | tf_op jit(solution)/shard_map/psum | solution.py:282
  480.7 2.3 convert_add_fusion
  483.0 169.1 %all-reduce.5.cloned.1.call-done = (f32[768,192]{0,1:T(8,128)}, f32[768,192]{0,1:T(8,128)}, f32[768,192]{0,1:T(8,128)}, f32[192,768]{1,0:T(8,128)}, f32[768,768]{1,0:T(8,128)}, /*index=5*/f32[768,768]{1,0:T(8,128)}) async-done(((f32[768,192]{0,1:T(8,128)}, f32[768,192]{0,1:T(8,128)}, f32[768,192]{0,1:T(8,128)}, f32[192,768]{1,0:T(8,128)}, f32[768,768]{1,0:T(8,128)}, /*index=5*/f32[768,768]{1,0:T(8,128)}), ...) | async-done | bytes 7077904 | tf_op jit(solution)/shard_map/psum | solution.py:282
  652.1 2.1 copy.123
  654.2 1.9 copy.124
  656.1 1.9 copy.125
  (154 shorter events, 31.2 us)
Async XLA Ops:
  7.2 141.2 %copy-start = (bf16[768,768]{1,0:T(8,128)(2,1)S(1)}, bf16[768,768]{1,0:T(8,128)(2,1)}, u32[]{:S(2)}) copy-start(bf16[768,768]{1,0:T(8,128)(2,1)} %param.33) | copy-start | bytes 3538948
  7.2 19.2 %copy-start.18 = (bf16[456,768]{1,0:T(8,128)(2,1)S(1)}, bf16[456,768]{1,0:T(8,128)(2,1)}, u32[]{:S(2)}) copy-start(bf16[456,768]{1,0:T(8,128)(2,1)} %param.20) | copy-start | bytes 2101252
  7.2 111.2 %reduce-scatter.5.cloned.1.call-start = ((), (), s32[]{:S(2)}) async-start(), calls=%async_computation.4 | async-start | bytes 7004160 | tf_op jit(solution)/shard_map/reduce_scatter | solution.py:137
  7.3 16.3 %collective-permute-start = (bf16[456,768]{1,0:T(8,128)(2,1)}, bf16[456,768]{1,0:T(8,128)(2,1)S(1)}, u32[]{:S(2)}, u32[]{:S(2)}) collective-permute-start(bf16[456,768]{1,0:T(8,128)(2,1)} %param.20), channel_id=1, source_target_pairs={{0,1},{1,2},{2,3},{3,0},{4,5},{5,6},{6,7},{7,4},{8,9},{9,10},{10,1... | collective-permute-start | bytes 2101256 | tf_op jit(solution)/shard_map/ppermute | solution.py:23
  7.8 18.8 %collective-permute-start.1 = (bf16[456,768]{1,0:T(8,128)(2,1)}, bf16[456,768]{1,0:T(8,128)(2,1)S(1)}, u32[]{:S(2)}, u32[]{:S(2)}) collective-permute-start(bf16[456,768]{1,0:T(8,128)(2,1)} %param.20), channel_id=1, source_target_pairs={{0,3},{1,0},{2,1},{3,2},{4,7},{5,4},{6,5},{7,6},{8,11},{9,8},{10,9... | collective-permute-start | bytes 2101256 | tf_op jit(solution)/shard_map/ppermute | solution.py:28
  23.6 10.5 %collective-permute-start.2 = (bf16[456,768]{1,0:T(8,128)(2,1)S(1)}, bf16[456,768]{1,0:T(8,128)(2,1)S(1)}, u32[]{:S(2)}, u32[]{:S(2)}) collective-permute-start(bf16[456,768]{1,0:T(8,128)(2,1)S(1)} %collective-permute-done), channel_id=1, source_target_pairs={{0,1},{1,2},{2,3},{3,0},{4,5},{5,6},{6,7},{7,4},{8,9},{9,10},{10,1... | collective-permute-start | bytes 2101256 | tf_op jit(solution)/shard_map/ppermute | solution.py:23
  26.4 9.3 %copy-start.26 = (bf16[768,192]{0,1:T(8,128)(2,1)S(1)}, bf16[768,192]{0,1:T(8,128)(2,1)}, u32[]{:S(2)}) copy-start(bf16[768,192]{0,1:T(8,128)(2,1)} %param.26) | copy-start | bytes 884740
  35.7 2.4 copy-start.40
  38.2 11.2 %copy-start.7 = (bf16[8,228,3,64]{1,0,3,2:T(8,128)(2,1)}, bf16[8,228,3,64]{1,0,3,2:T(8,128)(2,1)S(1)}, u32[]{:S(2)}) copy-start(bf16[8,228,3,64]{1,0,3,2:T(8,128)(2,1)S(1)} %reshape.129) | copy-start | bytes 2101252
  38.2 4.5 copy-start.41
  42.7 6.6 copy-start.9
  49.4 2.8 copy-start.16
  51.2 2.5 copy-start.2
  51.2 2.5 copy-start.22
  60.7 57.7 %copy-start.34 = (f32[768]{0:T(1024)S(1)}, f32[768]{0:T(1024)}, u32[]{:S(2)}) copy-start(f32[768]{0:T(1024)} %param.30) | copy-start | bytes 9220
  60.7 59.7 %copy-start.31 = (f32[768]{0:T(1024)S(1)}, f32[768]{0:T(1024)}, u32[]{:S(2)}) copy-start(f32[768]{0:T(1024)} %param.31) | copy-start | bytes 9220
  60.8 59.7 %copy-start.33 = (f32[768]{0:T(1024)S(1)}, f32[768]{0:T(1024)}, u32[]{:S(2)}) copy-start(f32[768]{0:T(1024)} %param.32) | copy-start | bytes 9220
  60.8 87.6 %all-gather.4.cloned.1.call-start = ((), (), s32[]{:S(2)}) async-start(), calls=%async_computation.5 | async-start | bytes 3502080 | tf_op jit(solution)/shard_map/all_gather | solution.py:150
  120.2 28.2 %copy-start.39 = (f32[768]{0:T(1024)S(1)}, f32[768]{0:T(1024)}, u32[]{:S(2)}) copy-start(f32[768]{0:T(1024)} %param.34) | copy-start | bytes 9220
  121.7 93.3 %reduce-scatter.7.cloned.1.call-start = ((), (), s32[]{:S(2)}) async-start(), calls=%async_computation.6 | async-start | bytes 7004160 | tf_op jit(solution)/shard_map/reduce_scatter | solution.py:154
  148.4 7.9 %copy-start.38 = (bf16[768,768]{1,0:T(8,128)(2,1)S(1)}, bf16[768,768]{1,0:T(8,128)(2,1)}, u32[]{:S(2)}) copy-start(bf16[768,768]{1,0:T(8,128)(2,1)} %param.35) | copy-start | bytes 3538948
  161.1 53.8 %copy-start.36 = (f32[768]{0:T(1024)S(1)}, f32[768]{0:T(1024)}, u32[]{:S(2)}) copy-start(f32[768]{0:T(1024)} %param.36) | copy-start | bytes 9220
  161.2 56.1 %copy-start.32 = (f32[768]{0:T(1024)S(1)}, f32[768]{0:T(1024)}, u32[]{:S(2)}) copy-start(f32[768]{0:T(1024)} %param.37) | copy-start | bytes 9220
  161.2 84.9 %all-gather.6.cloned.1.call-start = ((), (), s32[]{:S(2)}) async-start(), calls=%async_computation.7 | async-start | bytes 3502080 | tf_op jit(solution)/shard_map/all_gather | solution.py:213
  215.0 2.3 copy-start.13
  219.4 93.4 %reduce-scatter.9.cloned.1.call-start = ((), (), s32[]{:S(2)}) async-start(), calls=%async_computation.8 | async-start | bytes 7004160 | tf_op jit(solution)/shard_map/reduce_scatter | solution.py:222
  258.9 53.8 %copy-start.14 = (bf16[456,768]{1,0:T(8,128)(2,1)S(1)}, bf16[456,768]{1,0:T(8,128)(2,1)}, u32[]{:S(2)}) copy-start(bf16[456,768]{1,0:T(8,128)(2,1)} %param.39) | copy-start | bytes 2101252
  258.9 53.8 %copy-start.35 = (f32[768]{0:T(1024)S(1)}, f32[768]{0:T(1024)}, u32[]{:S(2)}) copy-start(f32[768]{0:T(1024)} %param.38) | copy-start | bytes 9220
  259.0 86.1 %all-gather.8.cloned.1.call-start = ((), (), s32[]{:S(2)}) async-start(), calls=%async_computation.9 | async-start | bytes 3502080 | tf_op jit(solution)/shard_map/all_gather | solution.py:246
  316.6 2.0 copy-start.23
  316.6 2.0 copy-start.30
  316.6 28.5 %copy-start.24 = (bf16[192,768]{1,0:T(8,128)(2,1)S(1)}, bf16[192,768]{1,0:T(8,128)(2,1)}, u32[]{:S(2)}) copy-start(bf16[192,768]{1,0:T(8,128)(2,1)} %param.29) | copy-start | bytes 884740
  318.4 162.3 %reduce-scatter.11.cloned.1.call-start = ((), (), s32[]{:S(2)}) async-start(), calls=%async_computation.10 | async-start | bytes 3502080 | tf_op jit(solution)/shard_map/reduce_scatter | solution.py:270
  349.3 4.0 copy-start.17
  349.3 8.4 %slice-start = ((s8[5701632]{0:T(1024)(128)(4,1)}), s8[4194304]{0:T(1024)(128)(4,1)S(1)}, s32[]{:S(2)}) async-start(s8[5701632]{0:T(1024)(128)(4,1)} %bitcast.68), calls=%async_computation.12 | async-start | bytes 8388608
  353.3 4.5 slice-start.1
  359.2 1.9 copy-start.8
  364.8 7.1 %copy-start.25 = (bf16[768,192]{0,1:T(8,128)(2,1)S(1)}, bf16[768,192]{0,1:T(8,128)(2,1)}, u32[]{:S(2)}) copy-start(bf16[768,192]{0,1:T(8,128)(2,1)} %param.24) | copy-start | bytes 884740
  376.7 275.4 %all-reduce.5.cloned.1.call-start = ((), (), s32[]{:S(2)}) async-start(), calls=%async_computation.11 | async-start | bytes 14155776 | tf_op jit(solution)/shard_map/psum | solution.py:282
  376.8 6.9 %copy-start.37 = (bf16[1824,768]{1,0:T(8,128)(2,1)S(1)}, bf16[1824,768]{1,0:T(8,128)(2,1)}, u32[]{:S(2)}) copy-start(bf16[1824,768]{1,0:T(8,128)(2,1)} %all-gather.4.cloned.1.call-done) | copy-start | bytes 8404996
  376.8 6.9 %copy-start.44 = (bf16[1824,768]{1,0:T(8,128)(2,1)S(1)}, bf16[1824,768]{1,0:T(8,128)(2,1)}, u32[]{:S(2)}) copy-start(bf16[1824,768]{1,0:T(8,128)(2,1)} %copy-done.43) | copy-start | bytes 8404996
  383.7 4.1 copy-start.4
  383.7 4.1 copy-start.12
  394.5 86.2 %copy-start.15 = (f32[456,768]{1,0:T(8,128)S(1)}, f32[456,768]{1,0:T(8,128)}, u32[]{:S(2)}) copy-start(f32[456,768]{1,0:T(8,128)} %get-tuple-element.41) | copy-start | bytes 4202500
  652.1 5.9 copy-start.21
  652.1 6.7 %copy-start.20 = (f32[768,768]{1,0:T(8,128)S(1)}, f32[768,768]{1,0:T(8,128)}, u32[]{:S(2)}) copy-start(f32[768,768]{1,0:T(8,128)} %get-tuple-element.73) | copy-start | bytes 7077892
  658.0 2.2 copy-start.19
  658.8 2.8 copy-start.1
  (10 other events, 13.5 us)
Sparse Core Ops, SparseCore 0:
  60.9 57.4 reduce-scatter.4
  121.8 26.5 all-gather.3
  161.3 53.6 reduce-scatter.6
  219.5 26.5 all-gather.5
  259.1 53.6 reduce-scatter.8
  318.5 26.5 all-gather.7
  376.9 36.2 reduce-scatter.10
  419.4 232.6 all-reduce.4
